TPU v7x, 32 devices: a whole 2x2x4 slice. The times are simulated.
32 devices in a mesh: tm: 4 (over z), rows: 8 (over y, x, core).
Axes of the slice: x: 2, y: 2, z: 4, core: 2. Of those that a mesh axis runs over, the one named last changes fastest.
Arguments:
- frames: bfloat16 [8, 16, 128, 256], P('tm', 'rows'), may hold values from -30 to 30
- frame_counts: int32 [4], replicated, may hold values from 0 to 2, as said below
- norm_gain: float32 [256], replicated, may hold values from 0.5 to 1.5
- norm_bias: float32 [256], replicated, may hold values from -3 to 3
- conv3_weight: bfloat16 [3, 3, 3, 256, 256], replicated, may hold values from -0.078125 to 0.078125
- conv3_bias: float32 [256], replicated, may hold values from -3 to 3
- conv2_weight: bfloat16 [3, 3, 256, 256], replicated, may hold values from -0.125 to 0.125
- conv2_bias: float32 [256], replicated, may hold values from -3 to 3
Outputs:
- decoded: bfloat16 [4, 32, 256, 256], P('tm', 'rows')
Inputs may be any that keep to these rules, and one draw needn't show every extreme that they name: `frame_counts`: device d of tm holds the frames starting at the sum of the counts before it, and its first frame index is d or d + 1; the counts sum to 4. Slots at or beyond a device's count hold values that belong to no frame.
All inputs are finite; a program needn't handle non-finite values.
Results may differ from a plain program's by a relative error of at most 0.005.
Values may be sent and summed in bfloat16 or wider, within the bound.
A program may use at most 64 MiB of HBM per device.

v0:
```python
import jax
import jax.numpy as jnp
from jax import lax
from jax.sharding import PartitionSpec as P

GROUPS = 32


norm_eps = 1e-06


def prefix(value, axis, join, neutral):
    count, mine = (lax.axis_size(axis), lax.axis_index(axis))
    pieces = jax.tree.map(lambda part: lax.all_gather(part, axis), value)
    running = jax.tree.map(
        lambda part, zero: jnp.full_like(part, 0) + jnp.asarray(zero, part.dtype), value, neutral
    )

    def step(position, running):
        longer = join(running, jax.tree.map(lambda part: part[position], pieces))
        return jax.tree.map(lambda new, old: jnp.where(position < mine, new, old), longer, running)

    return lax.fori_loop(0, count - 1, step, running)


def extended(block, sides, width):
    for axis, dim in sides:
        count = lax.axis_size(axis)
        forward = [(i, i + 1) for i in range(count - 1)]
        backward = [(target, source) for source, target in forward]
        low = lax.ppermute(
            lax.slice_in_dim(block, block.shape[dim] - width, None, axis=dim), axis, forward
        )
        high = lax.ppermute(lax.slice_in_dim(block, 0, width, axis=dim), axis, backward)
        block = jnp.concatenate([low, block, high], axis=dim)
    return block


def from_behind(value, axis, by):
    devices = lax.axis_size(axis)
    pairs = [(i, i + by) for i in range(devices) if 0 <= i + by < devices]
    return lax.ppermute(value, axis, pairs)


def widen(blocks):
    return jnp.pad(blocks, ((0, 0), (0, 0), (1, 1), (0, 0)))


def stencil(padded, kernel, frames_out, rows_out, columns):
    kernel_depth = kernel.shape[0]
    channels = padded.shape[-1]
    summed = jnp.zeros((frames_out * rows_out * columns, kernel.shape[-1]), jnp.float32)
    for tap_time in range(kernel_depth):
        for tap_row in range(3):
            joined = jnp.concatenate(
                [
                    padded[
                        tap_time : tap_time + frames_out,
                        tap_row : tap_row + rows_out,
                        tap_col : tap_col + columns,
                        :,
                    ]
                    for tap_col in range(3)
                ],
                axis=-1,
            )
            summed = summed + jnp.dot(
                joined.reshape(-1, 3 * channels),
                kernel[tap_time, tap_row].reshape(3 * channels, -1),
                preferred_element_type=jnp.float32,
            )
    return summed.reshape(frames_out, rows_out, columns, -1)


def keep_last(earlier, later):
    early_frames, early_count = earlier
    late_frames, late_count = later
    shifted = jnp.stack([early_frames[1], late_frames[1]])
    chosen = jnp.where(
        late_count >= 2, late_frames, jnp.where(late_count >= 1, shifted, early_frames)
    )
    return (chosen, jnp.minimum(early_count + late_count, 2).astype(late_count.dtype))


def decode(
    block, live_count, chan_scale, chan_shift, conv3_weight, conv3_bias, conv2_weight, conv2_bias
):
    values = block.astype(jnp.float32)
    hidden = jax.nn.silu(values * chan_scale + chan_shift).astype(jnp.bfloat16)
    slot_count = hidden.shape[0]
    row_count = block.shape[1]
    col_count = block.shape[2]
    newest = lax.dynamic_index_in_dim(
        hidden, jnp.clip(live_count - 1, 0, slot_count - 1), 0, keepdims=False
    )
    before = lax.dynamic_index_in_dim(
        hidden, jnp.clip(live_count - 2, 0, slot_count - 1), 0, keepdims=False
    )
    tail_frames = jnp.stack([jnp.where(live_count >= 2, before, newest), newest])
    tail_count = jnp.minimum(live_count, 2) * jnp.ones((), jnp.bfloat16)
    identity = (jnp.zeros_like(tail_frames), jnp.zeros((), jnp.bfloat16))
    prior_frames, prior_count = prefix((tail_frames, tail_count), "tm", keep_last, identity)
    first_frame = hidden[0]
    older_frame = jnp.where(
        prior_count >= 2, prior_frames[0], jnp.where(prior_count >= 1, prior_frames[1], first_frame)
    )
    newer_frame = jnp.where(prior_count >= 1, prior_frames[1], first_frame)
    stacked = jnp.concatenate([older_frame[None], newer_frame[None], hidden], axis=0)
    haloed = extended(stacked, (("rows", 1),), 1)
    conv_out = stencil(widen(haloed), conv3_weight, slot_count, row_count, col_count)
    merged = (values + conv_out + conv3_bias).astype(jnp.bfloat16)
    doubled = jnp.repeat(jnp.repeat(merged, 2, axis=1), 2, axis=2)
    upsampled = extended(doubled, (("rows", 1),), 1)
    result = stencil(widen(upsampled), conv2_weight[None], slot_count, 2 * row_count, 2 * col_count)
    return (result + conv2_bias).astype(jnp.bfloat16)


def body(
    frames, frame_counts, norm_gain, norm_bias, conv3_weight, conv3_bias, conv2_weight, conv2_bias
):
    tm_index = lax.axis_index("tm")
    slot_count, row_count, col_count, channels = frames.shape
    starts = jnp.cumsum(frame_counts) - frame_counts
    my_count = frame_counts[tm_index]
    my_start = starts[tm_index]
    live_slots = (jnp.arange(slot_count) < my_count).astype(jnp.float32)
    values = frames.astype(jnp.float32) * live_slots[:, None, None, None]
    width_group = channels // GROUPS
    group_sum = jnp.sum(values, axis=(0, 1, 2)).reshape(GROUPS, width_group).sum(axis=1)
    group_square = jnp.sum(values * values, axis=(0, 1, 2)).reshape(GROUPS, width_group).sum(axis=1)
    total_sum, total_square = lax.psum((group_sum, group_square), ("tm", "rows"))
    cell_total = float(
        lax.axis_size("tm") * lax.axis_size("rows") * row_count * col_count * width_group
    )
    group_mean = total_sum / cell_total
    inverse = lax.rsqrt(total_square / cell_total - group_mean * group_mean + norm_eps)
    chan_scale = jnp.repeat(inverse, width_group) * norm_gain
    chan_shift = norm_bias - jnp.repeat(group_mean * inverse, width_group) * norm_gain
    finished = decode(
        frames, my_count, chan_scale, chan_shift, conv3_weight, conv3_bias, conv2_weight, conv2_bias
    )
    passing = lax.dynamic_index_in_dim(
        finished, jnp.clip(tm_index + 1 - my_start, 0, slot_count - 1), 0
    )
    from_below = from_behind(passing, "tm", 1)
    own_frame = lax.dynamic_index_in_dim(
        finished, jnp.clip(tm_index - my_start, 0, slot_count - 1), 0
    )
    return jnp.where(my_start > tm_index, from_below, own_frame)


def solution(mesh):
    placed = (P("tm", "rows", None, None), P(), P(), P(), P(), P(), P(), P())
    return jax.shard_map(
        body, mesh=mesh, in_specs=placed, out_specs=P("tm", "rows", None, None), check_vma=False
    )
```

profile of v0, /device:TPU:1, one launch (start us, length us, event | category | flops | bytes accessed | tf_op | source)
XLA Modules:
  0.0 153.4 jit_solution(10153708313104688034)
XLA Ops:
  6.5 1.3 dynamic_slice.35
  7.8 0.6 compare_convert_fusion
  8.4 1.1 fusion.27
  10.0 40.5 %all-reduce.3 = (f32[32]{0:T(128)S(1)}, f32[32]{0:T(128)S(1)}) all-reduce(f32[32]{0:T(128)S(1)} %reduce_sum.37, f32[32]{0:T(128)S(1)} %reduce_sum.39), channel_id=1, replica_groups=mesh['tm'=4,'rows'=8] {'tm','rows'}, use_global_device_ids=true, to_apply=%region_3.4 | all-reduce | flops 64 | bytes 512 | tf_op jit(solution)/shard_map/psum | solution.py:131
  52.6 0.7 fusion.48
  53.3 1.1 fusion.36
  54.4 0.7 pad_maximum_fusion.13
  55.7 0.6 dynamic-slice
  56.3 0.7 dynamic-update-slice
  57.0 8.5 %all-reduce.2 = bf16[4]{0:T(256)(128)(2,1)S(1)} all-reduce(bf16[4]{0:T(256)(128)(2,1)S(1)} %dynamic-update-slice), channel_id=1, replica_groups=mesh['tm'=4,'rows'=8] {'tm'}, use_global_device_ids=true, to_apply=%add.2 | all-reduce | flops 4 | bytes 16
  65.7 0.6 dynamic_slice.34
  66.9 16.6 %all-gather.3.cloned.1.call-done = bf16[8,2,128,256]{3,2,1,0:T(8,128)(2,1)} async-done(((bf16[2,2,128,256]{3,2,1,0:T(8,128)(2,1)}), bf16[8,2,128,256]{3,2,1,0:T(8,128)(2,1)}) %all-gather.3.cloned.1.call-update) | async-done | bytes 1048592 | tf_op jit(solution)/shard_map/all_gather | solution.py:14
  83.5 14.1 %while.16 = (s32[]{:T(128)}, bf16[2,2,128,256]{3,2,1,0:T(8,128)(2,1)S(1)}, bf16[]{:T(256)}, s32[]{:T(128)}, bf16[4]{0:T(256)(128)(2,1)S(1)}, /*index=5*/bf16[4,2...) while((s32[]{:T(128)}, ...), condition=%wide.region_8.9_spmd.clone, body=%wide.region_7.8_spmd.clone.sunk | while | flops 786442 | bytes 2097345 | solution.py:23
  83.5 0.6 dynamic_slice.51
  85.5 0.9 dynamic-slice_bitcast_fusion.2
  86.4 1.1 fusion.75
  88.2 0.6 dynamic_slice.51
  90.2 0.9 dynamic-slice_bitcast_fusion.2
  91.1 1.1 fusion.75
  92.9 0.6 dynamic_slice.51
  94.9 0.9 dynamic-slice_bitcast_fusion.2
  95.8 1.1 fusion.75
  97.8 4.1 %collective-permute-start = (bf16[4,1,128,256]{3,2,1,0:T(8,128)(2,1)S(1)}, bf16[4,1,128,256]{3,2,1,0:T(8,128)(2,1)S(1)}, u32[]{:S(2)}, u32[]{:S(2)}) collective-permute-start(bf16[4,1,128,256]{3,2,1,0:T(8,128)(2,1)S(1)} %get-tuple-element.208), channel_id=1, source_target_pairs={{0,1},{1,2},{2,3},{3,4},{4,5},{5,6},{6,7},{8,9},{9,10},{10,11},{11... | collective-permute-start | bytes 786440 | tf_op jit(solution)/shard_map/ppermute | solution.py:31
  101.9 1.9 %collective-permute-start.1 = (bf16[4,1,128,256]{3,2,1,0:T(8,128)(2,1)S(1)}, bf16[4,1,128,256]{3,2,1,0:T(8,128)(2,1)S(1)}, u32[]{:S(2)}, u32[]{:S(2)}) collective-permute-start(bf16[4,1,128,256]{3,2,1,0:T(8,128)(2,1)S(1)} %get-tuple-element.209), channel_id=1, source_target_pairs={{1,0},{2,1},{3,2},{4,3},{5,4},{6,5},{7,6},{9,8},{10,9},{11,10},{12... | collective-permute-start | bytes 786440 | tf_op jit(solution)/shard_map/ppermute | solution.py:34
  103.8 2.2 %fusion.40 = (bf16[1,1,3,256,256]{4,3,2,1,0:T(8,128)(2,1)S(1)}, bf16[1,1,3,256,256]{4,3,2,1,0:T(8,128)(2,1)S(1)}, bf16[1,1,3,256,256]{4,3,2,1,0:T(8,128)(2,1)S(1...) fusion(bf16[3,3,3,256,256]{4,3,2,1,0:T(8,128)(2,1)} %param.14), kind=kLoop, calls=%fused_computation.88 | loop fusion | bytes 7077888 | tf_op jit(solution)/shard_map/slice | solution.py:69
  106.0 3.6 %collective-permute-done.1 = bf16[4,1,128,256]{3,2,1,0:T(8,128)(2,1)S(1)} collective-permute-done((bf16[4,1,128,256]{3,2,1,0:T(8,128)(2,1)S(1)}, bf16[4,1,128,256]{3,2,1,0:T(8,128)(2,1)S(1)}, u32[]{:S(2)}, u32[]{:S(2)}) %collective-permute-start.1) | collective-permute-done | bytes 262176 | tf_op jit(solution)/shard_map/ppermute | solution.py:34
  109.6 0.4 select_maximum_fusion
  110.1 0.9 fusion.43
  112.6 0.4 convolution_add_fusion.7
  113.7 0.4 convolution_add_fusion.4
  114.1 0.4 convolution_add_fusion.3
  115.5 0.5 broadcast_in_dim.29
  116.1 0.4 reshape.117
  116.5 0.9 fusion.44
  117.4 1.9 %collective-permute-start.2 = (bf16[2,1,256,256]{3,2,1,0:T(8,128)(2,1)}, bf16[2,1,256,256]{3,2,1,0:T(8,128)(2,1)S(1)}, u32[]{:S(2)}, u32[]{:S(2)}) collective-permute-start(bf16[2,1,256,256]{3,2,1,0:T(8,128)(2,1)} %get-tuple-element.198), channel_id=1, source_target_pairs={{0,1},{1,2},{2,3},{3,4},{4,5},{5,6},{6,7},{8,9},{9,10},{10,11},{11... | collective-permute-start | bytes 786440 | tf_op jit(solution)/shard_map/ppermute | solution.py:31
  119.3 2.6 %collective-permute-start.3 = (bf16[2,1,256,256]{3,2,1,0:T(8,128)(2,1)}, bf16[2,1,256,256]{3,2,1,0:T(8,128)(2,1)S(1)}, u32[]{:S(2)}, u32[]{:S(2)}) collective-permute-start(bf16[2,1,256,256]{3,2,1,0:T(8,128)(2,1)} %get-tuple-element.199), channel_id=1, source_target_pairs={{1,0},{2,1},{3,2},{4,3},{5,4},{6,5},{7,6},{9,8},{10,9},{11,10},{12... | collective-permute-start | bytes 786440 | tf_op jit(solution)/shard_map/ppermute | solution.py:34
  121.9 2.1 %fusion.42 = (bf16[1,1,3,256,256]{4,3,2,1,0:T(8,128)(2,1)S(1)}, bf16[1,1,3,256,256]{4,3,2,1,0:T(8,128)(2,1)S(1)}, bf16[1,1,3,256,256]{4,3,2,1,0:T(8,128)(2,1)}) fusion(bf16[1,3,3,256,256]{4,3,2,1,0:T(8,128)(2,1)} %bitcast.97), kind=kLoop, calls=%fused_computation.90 | loop fusion | bytes 2359296 | tf_op jit(solution)/shard_map/slice | solution.py:69
  124.0 1.2 concatenate.93
  125.2 2.9 %collective-permute-done.3 = bf16[2,1,256,256]{3,2,1,0:T(8,128)(2,1)S(1)} collective-permute-done((bf16[2,1,256,256]{3,2,1,0:T(8,128)(2,1)}, bf16[2,1,256,256]{3,2,1,0:T(8,128)(2,1)S(1)}, u32[]{:S(2)}, u32[]{:S(2)}) %collective-permute-start.3) | collective-permute-done | bytes 262176 | tf_op jit(solution)/shard_map/ppermute | solution.py:34
  128.1 0.4 fusion.19
  128.5 0.9 fusion.41
  129.4 0.7 fusion.6
  130.2 1.0 fusion.50
  131.5 1.2 fusion.7
  132.7 1.0 fusion.13
  133.9 3.1 %collective-permute-start.4 = (bf16[1,4,256,256]{3,2,1,0:T(8,128)(2,1)S(1)}, bf16[1,4,256,256]{3,2,1,0:T(8,128)(2,1)S(1)}, u32[]{:S(2)}, u32[]{:S(2)}) collective-permute-start(bf16[1,4,256,256]{3,2,1,0:T(8,128)(2,1)S(1)} %constant_dynamic-slice_fusion), channel_id=1, source_target_pairs={{0,8},{8,16},{16,24},{1,9},{9,17},{17,25},{2,10},{10,18},{18,26},{... | collective-permute-start | bytes 1572872 | tf_op jit(solution)/shard_map/ppermute | solution.py:42
  138.3 7.4 %collective-permute-done.4 = bf16[1,4,256,256]{3,2,1,0:T(8,128)(2,1)S(1)} collective-permute-done((bf16[1,4,256,256]{3,2,1,0:T(8,128)(2,1)S(1)}, bf16[1,4,256,256]{3,2,1,0:T(8,128)(2,1)S(1)}, u32[]{:S(2)}, u32[]{:S(2)}) %collective-permute-start.4) | collective-permute-done | bytes 524320 | tf_op jit(solution)/shard_map/ppermute | solution.py:42
  145.7 0.8 dynamic-slice_select_fusion
  (60 shorter events, 5.1 us)
Async XLA Ops:
  6.5 49.2 %copy-start.6 = (u32[32]{0:T(128)S(1)}, u32[32]{0:T(128)}, u32[]{:S(2)}) copy-start(u32[32]{0:T(128)} %constant.96) | copy-start | bytes 388
  6.5 59.0 %copy-start.5 = (s32[4]{0:T(128)S(1)}, s32[4]{0:T(128)}, u32[]{:S(2)}) copy-start(s32[4]{0:T(128)} %param.11) | copy-start | bytes 52
  6.5 77.0 %all-gather.3.cloned.1.call-start = ((), (), s32[]{:S(2)}) async-start(), calls=%async_computation | async-start | bytes 1310720 | tf_op jit(solution)/shard_map/all_gather | solution.py:14
  97.8 8.2 %collective-permute-start = (bf16[4,1,128,256]{3,2,1,0:T(8,128)(2,1)S(1)}, bf16[4,1,128,256]{3,2,1,0:T(8,128)(2,1)S(1)}, u32[]{:S(2)}, u32[]{:S(2)}) collective-permute-start(bf16[4,1,128,256]{3,2,1,0:T(8,128)(2,1)S(1)} %get-tuple-element.208), channel_id=1, source_target_pairs={{0,1},{1,2},{2,3},{3,4},{4,5},{5,6},{6,7},{8,9},{9,10},{10,11},{11... | collective-permute-start | bytes 786440 | tf_op jit(solution)/shard_map/ppermute | solution.py:31
  101.9 7.7 %collective-permute-start.1 = (bf16[4,1,128,256]{3,2,1,0:T(8,128)(2,1)S(1)}, bf16[4,1,128,256]{3,2,1,0:T(8,128)(2,1)S(1)}, u32[]{:S(2)}, u32[]{:S(2)}) collective-permute-start(bf16[4,1,128,256]{3,2,1,0:T(8,128)(2,1)S(1)} %get-tuple-element.209), channel_id=1, source_target_pairs={{1,0},{2,1},{3,2},{4,3},{5,4},{6,5},{7,6},{9,8},{10,9},{11,10},{12... | collective-permute-start | bytes 786440 | tf_op jit(solution)/shard_map/ppermute | solution.py:34
  114.5 1.0 copy-start
  114.5 0.9 copy-start.3
  117.4 7.8 %collective-permute-start.2 = (bf16[2,1,256,256]{3,2,1,0:T(8,128)(2,1)}, bf16[2,1,256,256]{3,2,1,0:T(8,128)(2,1)S(1)}, u32[]{:S(2)}, u32[]{:S(2)}) collective-permute-start(bf16[2,1,256,256]{3,2,1,0:T(8,128)(2,1)} %get-tuple-element.198), channel_id=1, source_target_pairs={{0,1},{1,2},{2,3},{3,4},{4,5},{5,6},{6,7},{8,9},{9,10},{10,11},{11... | collective-permute-start | bytes 786440 | tf_op jit(solution)/shard_map/ppermute | solution.py:31
  119.3 8.8 %collective-permute-start.3 = (bf16[2,1,256,256]{3,2,1,0:T(8,128)(2,1)}, bf16[2,1,256,256]{3,2,1,0:T(8,128)(2,1)S(1)}, u32[]{:S(2)}, u32[]{:S(2)}) collective-permute-start(bf16[2,1,256,256]{3,2,1,0:T(8,128)(2,1)} %get-tuple-element.199), channel_id=1, source_target_pairs={{1,0},{2,1},{3,2},{4,3},{5,4},{6,5},{7,6},{9,8},{10,9},{11,10},{12... | collective-permute-start | bytes 786440 | tf_op jit(solution)/shard_map/ppermute | solution.py:34
  130.2 1.2 copy-start.1
  130.2 1.3 copy-start.2
  132.7 1.0 copy-start.4
  133.9 11.7 %collective-permute-start.4 = (bf16[1,4,256,256]{3,2,1,0:T(8,128)(2,1)S(1)}, bf16[1,4,256,256]{3,2,1,0:T(8,128)(2,1)S(1)}, u32[]{:S(2)}, u32[]{:S(2)}) collective-permute-start(bf16[1,4,256,256]{3,2,1,0:T(8,128)(2,1)S(1)} %constant_dynamic-slice_fusion), channel_id=1, source_target_pairs={{0,8},{8,16},{16,24},{1,9},{9,17},{17,25},{2,10},{10,18},{18,26},{... | collective-permute-start | bytes 1572872 | tf_op jit(solution)/shard_map/ppermute | solution.py:42
Sparse Core Ops, SparseCore 0:
  55.3 28.1 all-gather.2
where the time goes:
time: 156 us; the launch traced here: 153 us
  blocking collectives  49 us (31%)
  waiting for transfers between devices  30.5 us (20%)
  local copies, waits for them, and re-layouts  18 us (12%)
  between operations  18 us (12%)
  starting transfers between devices  13.6 us (9%)
  other arithmetic  11.6 us (7%)
  matrix products  6.53 us (4%)
  loops' own time  6.09 us (4%)
    psum x1, blocking collectives, body(): lax.psum((group_sum, group_square), ('tm', 'rows'))  40.5 us
    all_gather x1, waiting for transfers between devices, prefix(): pieces = jax.tree.map(lambda part: lax.all_gather(part, axis), value)  16.6 us
    unnamed x1, blocking collectives  8.52 us
    ppermute x1, waiting for transfers between devices, from_behind(): return lax.ppermute(value, axis, pairs)  7.37 us
    ppermute x2, waiting for transfers between devices, extended(): lax.ppermute(lax.slice_in_dim(block, 0, width, axis=dim), axis, backward)  6.55 us
    dot_general x12, matrix products, stencil(): jnp.dot(joined.reshape(-1, 3 * channels), kernel[tap_time, tap_row].resha...  6.53 us
    another operation x1, loops' own time, prefix(): return lax.fori_loop(0, count - 1, step, running)  6.09 us
    ppermute x2, starting transfers between devices, extended(): lax.ppermute(lax.slice_in_dim(block, block.shape[dim] - width, None, axis...  6 us
  transfers between devices with their start and end apart: 6, of which 4 were waited for; matrix products, arithmetic and copies ran while one was open for 5% of the time, Pallas kernels for 0%

commit v1 on v0

v1 whole, which is shorter than its diff:
```python
import functools

import jax
import jax.numpy as jnp
from jax import lax
from jax.experimental import pallas as pl
from jax.experimental.pallas import tpu as pltpu
from jax.sharding import PartitionSpec as P

GROUPS = 32
norm_eps = 1e-06
MESH = pl.DeviceIdType.MESH
f32 = jnp.float32
bf16 = jnp.bfloat16


def roll_rows(value, shift):
    return pltpu.roll(value, shift % value.shape[0], 0)


def side_by_side(value):
    columns = value.shape[0]
    place = lax.broadcasted_iota(jnp.int32, value.shape, 0)
    left = jnp.where(place == 0, 0.0, roll_rows(value, 1))
    right = jnp.where(place == columns - 1, 0.0, roll_rows(value, -1))
    return left, value, right


def group_total(value, width):
    channels = value.shape[1]
    lane = lax.broadcasted_iota(jnp.int32, value.shape, 1)
    step = 1
    while step < width:
        up = pltpu.roll(value, step, 1)
        down = pltpu.roll(value, channels - step, 1)
        value = value + jnp.where((lane // step) % 2 == 1, up, down)
        step *= 2
    return value


def kernel(
    n_tm, n_rows,
    counts, frames, gain, bias, w3_hbm, b3, w2_hbm, b2,
    out,
    w3, w2, cw, xsel, xgot, ext, joined, acc, mjoined, spread,
    mine, row_stats, plane, tm_stats,
    w_sem, sx, rx, sg, rg, sr, rr, s1, r1, s2, r2,
):
    band, columns, channels = frames.shape[1:]
    d = lax.axis_index("tm")
    r = lax.axis_index("rows")

    load3 = pltpu.make_async_copy(w3_hbm, w3, w_sem.at[0])
    load2 = pltpu.make_async_copy(w2_hbm, w2, w_sem.at[1])
    load2.start()
    load3.start()

    barrier = pltpu.get_barrier_semaphore()
    for k in range(1, n_rows):
        pl.semaphore_signal(
            barrier, inc=1, device_id={"rows": lax.rem(r + k, n_rows)}, device_id_type=MESH
        )
    for k in range(1, n_tm):
        pl.semaphore_signal(
            barrier, inc=1, device_id={"tm": lax.rem(d + k, n_tm)}, device_id_type=MESH
        )

    start = jnp.int32(0)
    for i in range(n_tm):
        start = start + jnp.where(i < d, counts[i], 0)
    live = counts[d]
    own_first = start == d

    for row in range(band):
        xsel[row] = jnp.where(own_first, frames[1, row], frames[0, row])
    total = jnp.zeros((8, channels), f32)
    square = jnp.zeros((8, channels), f32)
    for slot in range(frames.shape[0]):
        for row in range(band):
            value = jnp.where(slot < live, frames[slot, row].astype(f32), 0.0)
            value = value.reshape(columns // 8, 8, channels)
            total = total + jnp.sum(value, axis=0)
            square = square + jnp.sum(value * value, axis=0)
    total = jnp.sum(total, axis=0, keepdims=True)
    square = jnp.sum(square, axis=0, keepdims=True)
    mine[...] = jnp.concatenate(
        [jnp.broadcast_to(total, (4, channels)), jnp.broadcast_to(square, (4, channels))], axis=0
    )
    pl.semaphore_wait(barrier, n_rows - 1 + n_tm - 1)

    def x_copy(row):
        return pltpu.make_async_remote_copy(
            src_ref=xsel.at[row], dst_ref=xgot.at[row], send_sem=sx.at[row], recv_sem=rx.at[row],
            device_id={"tm": lax.rem(d + 1, n_tm)}, device_id_type=MESH,
        )

    def g_copy(frame, row):
        return pltpu.make_async_remote_copy(
            src_ref=ext.at[frame, band + row], dst_ref=ext.at[frame - 1, band + row],
            send_sem=sg.at[frame - 1, row], recv_sem=rg.at[frame - 1, row],
            device_id={"tm": lax.rem(d + 1, n_tm)}, device_id_type=MESH,
        )

    def r_copy(frame, row, down):
        target = lax.rem(r + (1 if down else n_rows - 1), n_rows)
        return pltpu.make_async_remote_copy(
            src_ref=ext.at[frame, band + row],
            dst_ref=ext.at[frame, (0 if down else 2 * band) + row],
            send_sem=sr.at[frame, row, down], recv_sem=rr.at[frame, row, down],
            device_id={"rows": target}, device_id_type=MESH,
        )

    has_next, has_last = d < n_tm - 1, d > 0
    has_above, has_below = r > 0, r < n_rows - 1
    edge_up = range(2)
    edge_down = range(band - 2, band)

    def stat1(k):
        return pltpu.make_async_remote_copy(
            src_ref=mine, dst_ref=row_stats.at[k - 1], send_sem=s1.at[k - 1], recv_sem=r1.at[k - 1],
            device_id={"rows": lax.rem(r + k, n_rows)}, device_id_type=MESH,
        )

    def stat2(k):
        return pltpu.make_async_remote_copy(
            src_ref=plane, dst_ref=tm_stats.at[k - 1], send_sem=s2.at[k - 1], recv_sem=r2.at[k - 1],
            device_id={"tm": lax.rem(d + k, n_tm)}, device_id_type=MESH,
        )

    for k in range(1, n_rows):
        stat1(k).start()

    @pl.when(has_next)
    def _():
        for row in range(band):
            x_copy(row).start()

    load2.wait()
    for phase_row in range(2):
        for tap_row in range(2):
            for phase_col in range(2):
                for tap_col in range(2):
                    rows_of = ((0,), (1, 2)) if phase_row == 0 else ((0, 1), (2,))
                    cols_of = ((0,), (1, 2)) if phase_col == 0 else ((0, 1), (2,))
                    summed = None
                    for a in rows_of[tap_row]:
                        for b in cols_of[tap_col]:
                            part = w2[a, b].astype(f32)
                            summed = part if summed is None else summed + part
                    cw[phase_row, tap_row, phase_col, pl.ds(tap_col * channels, channels), :] = (
                        summed.astype(bf16)
                    )

    for k in range(1, n_rows):
        stat1(k).wait_recv()
    plane_sum = mine[...]
    for k in range(1, n_rows):
        plane_sum = plane_sum + row_stats[k - 1]
    plane[...] = plane_sum

    def send_rows(frame, row):
        @pl.when(has_above)
        def _():
            if row in edge_up:
                r_copy(frame, row, 0).start()

        @pl.when(has_below)
        def _():
            if row in edge_down:
                r_copy(frame, row, 1).start()

    for row in range(band):
        @pl.when(has_last)
        def _():
            x_copy(row).wait_recv()
            ext[2, band + row] = jnp.where(own_first, frames[0, row], xgot[row])

        @pl.when(d == 0)
        def _():
            ext[2, band + row] = frames[0, row]
            ext[1, band + row] = frames[0, row]
            ext[0, band + row] = frames[0, row]

        if row == 0:
            for k in range(1, n_tm):
                stat2(k).start()

        @pl.when(has_next)
        def _():
            g_copy(2, row).start()

        send_rows(2, row)

    for row in range(band):
        @pl.when(has_last)
        def _():
            g_copy(2, row).wait_recv()

        @pl.when(has_next)
        def _():
            g_copy(1, row).start()

        send_rows(1, row)

    for k in range(1, n_tm):
        stat2(k).wait_recv()
    whole = plane[...]
    for k in range(1, n_tm):
        whole = whole + tm_stats[k - 1]
    width = channels // GROUPS
    whole = group_total(whole, width) / float(n_tm * n_rows * band * columns * width)
    mean, mean_square = whole[0:1], whole[4:5]
    inverse = lax.rsqrt(mean_square - mean * mean + norm_eps)
    scale = inverse * gain[...]
    shift = bias[...] - mean * inverse * gain[...]

    def hide(frame, j):
        value = ext[frame, band - 2 + j].astype(f32) * scale + shift
        value = 0.5 * value * (1.0 + jnp.tanh(0.5 * value))
        place = r * band + j - 2
        value = jnp.where((place >= 0) & (place < n_rows * band), value, 0.0)
        for i, part in enumerate(side_by_side(value)):
            joined[frame, pl.ds(j * columns, columns), pl.ds(i * channels, channels)] = (
                part.astype(bf16)
            )

    def wait_rows(frame):
        @pl.when(has_below)
        def _():
            for row in edge_up:
                r_copy(frame, row, 0).wait_recv()

        @pl.when(has_above)
        def _():
            for row in edge_down:
                r_copy(frame, row, 1).wait_recv()

    def taps(frame):
        depth = (band + 2) * columns
        summed = None
        for k in range(3):
            part = jnp.dot(
                joined[frame, pl.ds(k * columns, depth), :], w3[frame, k],
                preferred_element_type=f32,
            )
            summed = part if summed is None else summed + part
        return summed

    own = range(2, band + 2)
    halo = [j for j in range(band + 4) if j not in own]

    for j in own:
        hide(2, j)
    for j in own:
        hide(1, j)
    for row in range(band):
        @pl.when(has_last)
        def _():
            g_copy(1, row).wait_recv()

        send_rows(0, row)
    wait_rows(2)
    for j in halo:
        hide(2, j)
    load3.wait()
    acc[...] = taps(2)
    for j in own:
        hide(0, j)
    wait_rows(1)
    for j in halo:
        hide(1, j)
    acc[...] += taps(1)
    wait_rows(0)
    for j in halo:
        hide(0, j)
    acc[...] += taps(0)

    for j in range(band + 2):
        value = ext[2, band - 1 + j].astype(f32) + acc[pl.ds(j * columns, columns), :] + b3[...]
        place = r * band + j - 1
        value = jnp.where((place >= 0) & (place < n_rows * band), value, 0.0)
        for i, part in enumerate(side_by_side(value)):
            mjoined[pl.ds(j * columns, columns), pl.ds(i * channels, channels)] = part.astype(bf16)

    for p in range(2):
        for q in range(2):
            summed = b2[...]
            for t in range(2):
                summed = summed + jnp.dot(
                    mjoined[pl.ds((p + t) * columns, band * columns), pl.ds(q * channels, 2 * channels)],
                    cw[p, t, q], preferred_element_type=f32,
                )
            for i in range(band):
                for lane in range(0, channels, 128):
                    spread[2 * i + p, lane // 128, pl.ds(q, columns, stride=2), :] = (
                        summed[i * columns : (i + 1) * columns, lane : lane + 128]
                    )
        for i in range(band):
            for lane in range(0, channels, 128):
                out[2 * i + p, :, pl.ds(lane, 128)] = spread[2 * i + p, lane // 128].astype(bf16)

    for k in range(1, n_rows):
        stat1(k).wait_send()
    for k in range(1, n_tm):
        stat2(k).wait_send()

    @pl.when(has_next)
    def _():
        for row in range(band):
            x_copy(row).wait_send()
            g_copy(2, row).wait_send()
            g_copy(1, row).wait_send()

    @pl.when(has_above)
    def _():
        for frame in range(3):
            for row in edge_up:
                r_copy(frame, row, 0).wait_send()

    @pl.when(has_below)
    def _():
        for frame in range(3):
            for row in edge_down:
                r_copy(frame, row, 1).wait_send()


def body(
    frames, frame_counts, norm_gain, norm_bias, conv3_weight, conv3_bias, conv2_weight, conv2_bias
):
    n_tm, n_rows = lax.axis_size("tm"), lax.axis_size("rows")
    _, band, columns, channels = frames.shape
    vmem = pl.BlockSpec(memory_space=pltpu.VMEM)
    anywhere = pl.BlockSpec(memory_space=pl.ANY)
    dma = pltpu.SemaphoreType.DMA
    return pl.pallas_call(
        functools.partial(kernel, n_tm, n_rows),
        out_shape=jax.ShapeDtypeStruct((1, 2 * band, 2 * columns, channels), bf16),
        in_specs=[
            pl.BlockSpec(memory_space=pltpu.SMEM), vmem, vmem, vmem, anywhere, vmem, anywhere, vmem
        ],
        out_specs=pl.BlockSpec((None, 2 * band, 2 * columns, channels), lambda: (0, 0, 0, 0)),
        scratch_shapes=[
            pltpu.VMEM((3, 3, 3 * channels, channels), bf16),
            pltpu.VMEM((3, 3, channels, channels), bf16),
            pltpu.VMEM((2, 2, 2, 2 * channels, channels), bf16),
            pltpu.VMEM((band, columns, channels), bf16),
            pltpu.VMEM((band, columns, channels), bf16),
            pltpu.VMEM((3, 3 * band, columns, channels), bf16),
            pltpu.VMEM((3, (band + 4) * columns, 3 * channels), bf16),
            pltpu.VMEM(((band + 2) * columns, channels), f32),
            pltpu.VMEM(((band + 2) * columns, 3 * channels), bf16),
            pltpu.VMEM((2 * band, channels // 128, 2 * columns, 128), f32),
            pltpu.VMEM((8, channels), f32),
            pltpu.VMEM((n_rows - 1, 8, channels), f32),
            pltpu.VMEM((8, channels), f32),
            pltpu.VMEM((n_tm - 1, 8, channels), f32),
            dma((2,)),
            dma((band,)), dma((band,)),
            dma((2, band)), dma((2, band)),
            dma((3, band, 2)), dma((3, band, 2)),
            dma((n_rows - 1,)), dma((n_rows - 1,)),
            dma((n_tm - 1,)), dma((n_tm - 1,)),
        ],
        compiler_params=pltpu.CompilerParams(collective_id=0, has_side_effects=True),
        name="decoder_section",
    )(
        frame_counts, frames, norm_gain[None], norm_bias[None],
        conv3_weight.reshape(3, 3, 3 * channels, channels), conv3_bias[None],
        conv2_weight, conv2_bias[None],
    )


def solution(mesh):
    placed = (P("tm", "rows", None, None), P(), P(), P(), P(), P(), P(), P())
    return jax.shard_map(
        body, mesh=mesh, in_specs=placed, out_specs=P("tm", "rows", None, None), check_vma=False
    )
```

time: 156 us -> 25.7 us (0.16); the launches traced: 153 us -> 25.5 us
  blocking collectives: 49 us -> 0 us
  waiting for transfers between devices: 30.5 us -> 0 us
  Pallas kernels: 0 us -> 23.6 us
  between operations: 18 us -> 0.01 us
  local copies, waits for them, and re-layouts: 18 us -> 1.87 us
  starting transfers between devices: 13.6 us -> 0 us
  other arithmetic: 11.6 us -> 0 us
  matrix products: 6.53 us -> 0 us
  loops' own time: 6.09 us -> 0 us
    psum x1 -> x0, blocking collectives: 40.5 us -> none  [body(): lax.psum((group_sum, group_square), ('tm', 'rows'))]
    pallas_call x0 -> x1, Pallas kernels: none -> 23.6 us  [body(): pl.pallas_call(functools.partial(kernel, n_tm, n_rows), out_shape=jax.Sha...]
    all_gather x1 -> x0, waiting for transfers between devices: 16.6 us -> none  [prefix(): pieces = jax.tree.map(lambda part: lax.all_gather(part, axis), value)]
    ppermute x5 -> x0, waiting for transfers between devices: 13.9 us -> none  [the longest x1 7.37 us: from_behind(): return lax.ppermute(value, axis, pairs)]
    ppermute x5 -> x0, starting transfers between devices: 13.6 us -> none  [the longest x2 6 us: extended(): lax.ppermute(lax.slice_in_dim(block, block.shape[dim] - width, None, axis...]
    slice x13 -> x0, local copies, waits for them, and re-layouts: 9.87 us -> none  [the longest x2 4.24 us: stencil(): kernel[tap_time, tap_row].reshape(3 * channels, -1)]
    unnamed x1 -> x0, blocking collectives: 8.52 us -> none
    dot_general x12 -> x0, matrix products: 6.53 us -> none  [stencil(): jnp.dot(joined.reshape(-1, 3 * channels), kernel[tap_time, tap_row].resha...]
  transfers between devices with their start and end apart: 6 -> 0, of which waited for: 4 -> 0; matrix products, arithmetic and copies ran while one was open for 5% -> 0% of each run, Pallas kernels for 0% -> 0%
where the time goes in v1:
time: 25.7 us; the launch traced here: 25.5 us
  Pallas kernels  23.6 us (92%)
  local copies, waits for them, and re-layouts  1.87 us (7%)
    pallas_call x1, Pallas kernels, body(): pl.pallas_call(functools.partial(kernel, n_tm, n_rows), out_shape=jax.Sha...  23.6 us
    unnamed x1, local copies, waits for them, and re-layouts  1.87 us

profile of v1, /device:TPU:1, one launch (start us, length us, event | category | flops | bytes accessed | tf_op | source)
XLA Modules:
  0.0 25.5 jit_solution(13833375111142707598)
XLA Ops:
  0.0 23.6 %decoder_section.1 = bf16[1,4,256,256]{3,2,1,0:T(8,128)(2,1)} custom-call(s32[4]{0:T(128)} %counts.1, bf16[2,2,128,256]{3,2,1,0:T(8,128)(2,1)} %frames.1, f32[1,256]{1,0:T(1,128)} %bitcast.6, f32[1,256]{1,0:T(1,128)} %bitcast.7, bf16[3,3,768,256]{3,2,1,0:T(8,128)(2,1)} %bitcast.5, f32[1,256]{1,0:T(1,128)} %bitcast.8, bf16[3,3,256,256]{3,2,1,0:T(8,128)(2,1)} %w2_hbm.1, ...), custom_call_target="tpu_custom_call" | custom-call | tf_op jit(solution)/shard_map/decoder_section/pallas_call | solution.py:335
  23.6 1.9 %copy.10 = bf16[1,4,256,256]{3,2,1,0:T(8,128)(2,1)} copy(bf16[1,4,256,256]{3,2,1,0:T(8,128)(2,1)} %decoder_section.1) | data formatting | bytes 1048576

commit v2 on v1

--- a/solution.py
+++ b/solution.py
@@ -40,20 +40,16 @@
 
 def kernel(
     n_tm, n_rows,
-    counts, frames, gain, bias, w3_hbm, b3, w2_hbm, b2,
+    counts_hbm, frames_hbm, gain_hbm, bias_hbm, w3_hbm, b3_hbm, w2_hbm, b2_hbm,
     out,
+    counts, frames, gain, bias, b3, b2,
     w3, w2, cw, xsel, xgot, ext, joined, acc, mjoined, spread,
     mine, row_stats, plane, tm_stats,
     w_sem, sx, rx, sg, rg, sr, rr, s1, r1, s2, r2,
 ):
-    band, columns, channels = frames.shape[1:]
+    band, columns, channels = frames_hbm.shape[1:]
     d = lax.axis_index("tm")
     r = lax.axis_index("rows")
-
-    load3 = pltpu.make_async_copy(w3_hbm, w3, w_sem.at[0])
-    load2 = pltpu.make_async_copy(w2_hbm, w2, w_sem.at[1])
-    load2.start()
-    load3.start()
 
     barrier = pltpu.get_barrier_semaphore()
     for k in range(1, n_rows):
@@ -64,6 +60,25 @@
         pl.semaphore_signal(
             barrier, inc=1, device_id={"tm": lax.rem(d + k, n_tm)}, device_id_type=MESH
         )
+
+    load_counts = pltpu.make_async_copy(counts_hbm, counts, w_sem.at[2])
+    load_frames = pltpu.make_async_copy(frames_hbm, frames, w_sem.at[3])
+    load3 = pltpu.make_async_copy(w3_hbm, w3, w_sem.at[0])
+    load2 = pltpu.make_async_copy(w2_hbm, w2, w_sem.at[1])
+    small = [
+        pltpu.make_async_copy(source, target, w_sem.at[4 + i])
+        for i, (source, target) in enumerate(
+            ((gain_hbm, gain), (bias_hbm, bias), (b3_hbm, b3), (b2_hbm, b2))
+        )
+    ]
+    load_counts.start()
+    load_frames.start()
+    load2.start()
+    load3.start()
+    for load in small:
+        load.start()
+    load_counts.wait()
+    load_frames.wait()
 
     start = jnp.int32(0)
     for i in range(n_tm):
@@ -73,9 +88,55 @@
 
     for row in range(band):
         xsel[row] = jnp.where(own_first, frames[1, row], frames[0, row])
+    pl.semaphore_wait(barrier, n_rows - 1 + n_tm - 1)
+
+    def x_copy(row):
+        return pltpu.make_async_remote_copy(
+            src_ref=xsel.at[row], dst_ref=xgot.at[row], send_sem=sx.at[row], recv_sem=rx.at[row],
+            device_id={"tm": lax.rem(d + 1, n_tm)}, device_id_type=MESH,
+        )
+
+    def g_copy(frame, row):
+        return pltpu.make_async_remote_copy(
+            src_ref=ext.at[frame, band + row], dst_ref=ext.at[frame - 1, band + row],
+            send_sem=sg.at[frame - 1, row], recv_sem=rg.at[frame - 1, row],
+            device_id={"tm": lax.rem(d + 1, n_tm)}, device_id_type=MESH,
+        )
+
+    def r_copy(frame, row, down):
+        target = lax.rem(r + (1 if down else n_rows - 1), n_rows)
+        return pltpu.make_async_remote_copy(
+            src_ref=ext.at[frame, band + row],
+            dst_ref=ext.at[frame, (0 if down else 2 * band) + row],
+            send_sem=sr.at[frame, row, down], recv_sem=rr.at[frame, row, down],
+            device_id={"rows": target}, device_id_type=MESH,
+        )
+
+    has_next, has_last = d < n_tm - 1, d > 0
+    has_above, has_below = r > 0, r < n_rows - 1
+    edge_up = range(2)
+    edge_down = range(band - 2, band)
+
+    def stat1(k):
+        return pltpu.make_async_remote_copy(
+            src_ref=mine, dst_ref=row_stats.at[k - 1], send_sem=s1.at[k - 1], recv_sem=r1.at[k - 1],
+            device_id={"rows": lax.rem(r + k, n_rows)}, device_id_type=MESH,
+        )
+
+    def stat2(k):
+        return pltpu.make_async_remote_copy(
+            src_ref=plane, dst_ref=tm_stats.at[k - 1], send_sem=s2.at[k - 1], recv_sem=r2.at[k - 1],
+            device_id={"tm": lax.rem(d + k, n_tm)}, device_id_type=MESH,
+        )
+
+    @pl.when(has_next)
+    def _():
+        for row in range(band):
+            x_copy(row).start()
+
     total = jnp.zeros((8, channels), f32)
     square = jnp.zeros((8, channels), f32)
-    for slot in range(frames.shape[0]):
+    for slot in range(frames_hbm.shape[0]):
         for row in range(band):
             value = jnp.where(slot < live, frames[slot, row].astype(f32), 0.0)
             value = value.reshape(columns // 8, 8, channels)
@@ -86,54 +147,8 @@
     mine[...] = jnp.concatenate(
         [jnp.broadcast_to(total, (4, channels)), jnp.broadcast_to(square, (4, channels))], axis=0
     )
-    pl.semaphore_wait(barrier, n_rows - 1 + n_tm - 1)
-
-    def x_copy(row):
-        return pltpu.make_async_remote_copy(
-            src_ref=xsel.at[row], dst_ref=xgot.at[row], send_sem=sx.at[row], recv_sem=rx.at[row],
-            device_id={"tm": lax.rem(d + 1, n_tm)}, device_id_type=MESH,
-        )
-
-    def g_copy(frame, row):
-        return pltpu.make_async_remote_copy(
-            src_ref=ext.at[frame, band + row], dst_ref=ext.at[frame - 1, band + row],
-            send_sem=sg.at[frame - 1, row], recv_sem=rg.at[frame - 1, row],
-            device_id={"tm": lax.rem(d + 1, n_tm)}, device_id_type=MESH,
-        )
-
-    def r_copy(frame, row, down):
-        target = lax.rem(r + (1 if down else n_rows - 1), n_rows)
-        return pltpu.make_async_remote_copy(
-            src_ref=ext.at[frame, band + row],
-            dst_ref=ext.at[frame, (0 if down else 2 * band) + row],
-            send_sem=sr.at[frame, row, down], recv_sem=rr.at[frame, row, down],
-            device_id={"rows": target}, device_id_type=MESH,
-        )
-
-    has_next, has_last = d < n_tm - 1, d > 0
-    has_above, has_below = r > 0, r < n_rows - 1
-    edge_up = range(2)
-    edge_down = range(band - 2, band)
-
-    def stat1(k):
-        return pltpu.make_async_remote_copy(
-            src_ref=mine, dst_ref=row_stats.at[k - 1], send_sem=s1.at[k - 1], recv_sem=r1.at[k - 1],
-            device_id={"rows": lax.rem(r + k, n_rows)}, device_id_type=MESH,
-        )
-
-    def stat2(k):
-        return pltpu.make_async_remote_copy(
-            src_ref=plane, dst_ref=tm_stats.at[k - 1], send_sem=s2.at[k - 1], recv_sem=r2.at[k - 1],
-            device_id={"tm": lax.rem(d + k, n_tm)}, device_id_type=MESH,
-        )
-
     for k in range(1, n_rows):
         stat1(k).start()
-
-    @pl.when(has_next)
-    def _():
-        for row in range(band):
-            x_copy(row).start()
 
     load2.wait()
     for phase_row in range(2):
@@ -151,13 +166,6 @@
                         summed.astype(bf16)
                     )
 
-    for k in range(1, n_rows):
-        stat1(k).wait_recv()
-    plane_sum = mine[...]
-    for k in range(1, n_rows):
-        plane_sum = plane_sum + row_stats[k - 1]
-    plane[...] = plane_sum
-
     def send_rows(frame, row):
         @pl.when(has_above)
         def _():
@@ -181,15 +189,21 @@
             ext[1, band + row] = frames[0, row]
             ext[0, band + row] = frames[0, row]
 
+        @pl.when(has_next)
+        def _():
+            g_copy(2, row).start()
+
+        send_rows(2, row)
+
         if row == 0:
+            for k in range(1, n_rows):
+                stat1(k).wait_recv()
+            plane_sum = mine[...]
+            for k in range(1, n_rows):
+                plane_sum = plane_sum + row_stats[k - 1]
+            plane[...] = plane_sum
             for k in range(1, n_tm):
                 stat2(k).start()
-
-        @pl.when(has_next)
-        def _():
-            g_copy(2, row).start()
-
-        send_rows(2, row)
 
     for row in range(band):
         @pl.when(has_last)
@@ -211,8 +225,13 @@
     whole = group_total(whole, width) / float(n_tm * n_rows * band * columns * width)
     mean, mean_square = whole[0:1], whole[4:5]
     inverse = lax.rsqrt(mean_square - mean * mean + norm_eps)
+    for load in small:
+        load.wait()
     scale = inverse * gain[...]
     shift = bias[...] - mean * inverse * gain[...]
+
+    def slot_of(j):
+        return j - 2 if 2 <= j < band + 2 else j + band if j < 2 else j
 
     def hide(frame, j):
         value = ext[frame, band - 2 + j].astype(f32) * scale + shift
@@ -220,7 +239,7 @@
         place = r * band + j - 2
         value = jnp.where((place >= 0) & (place < n_rows * band), value, 0.0)
         for i, part in enumerate(side_by_side(value)):
-            joined[frame, pl.ds(j * columns, columns), pl.ds(i * channels, channels)] = (
+            joined[frame, pl.ds(slot_of(j) * columns, columns), pl.ds(i * channels, channels)] = (
                 part.astype(bf16)
             )
 
@@ -235,48 +254,60 @@
             for row in edge_down:
                 r_copy(frame, row, 1).wait_recv()
 
-    def taps(frame):
-        depth = (band + 2) * columns
-        summed = None
+    def tap(frame, k, first, rows):
+        return jnp.dot(
+            joined[frame, pl.ds(first * columns, rows * columns), :], w3[frame, k],
+            preferred_element_type=f32,
+        )
+
+    def own_taps(frame):
         for k in range(3):
-            part = jnp.dot(
-                joined[frame, pl.ds(k * columns, depth), :], w3[frame, k],
-                preferred_element_type=f32,
-            )
-            summed = part if summed is None else summed + part
-        return summed
+            acc[pl.ds((2 - k) * columns, band * columns), :] += tap(frame, k, 0, band)
+
+    def halo_taps(frame):
+        acc[pl.ds(0, 2 * columns), :] += tap(frame, 0, band, 2)
+        acc[pl.ds(band * columns, 2 * columns), :] += tap(frame, 2, band + 2, 2)
+        middle = tap(frame, 1, band + 1, 2)
+        acc[pl.ds(0, columns), :] += middle[:columns]
+        acc[pl.ds((band + 1) * columns, columns), :] += middle[columns:]
 
     own = range(2, band + 2)
     halo = [j for j in range(band + 4) if j not in own]
 
-    for j in own:
-        hide(2, j)
-    for j in own:
-        hide(1, j)
-    for row in range(band):
+    def hide_rows(frame, rows):
+        for j in rows:
+            hide(frame, j)
+
+    def older(row):
         @pl.when(has_last)
         def _():
             g_copy(1, row).wait_recv()
 
         send_rows(0, row)
+
+    acc[...] = jnp.zeros(acc.shape, f32) + b3[...]
+    hide_rows(2, own)
+    load3.wait()
+    own_taps(2)
+    hide_rows(1, own)
+    older(0)
     wait_rows(2)
-    for j in halo:
-        hide(2, j)
-    load3.wait()
-    acc[...] = taps(2)
-    for j in own:
-        hide(0, j)
+    hide_rows(2, halo)
+    halo_taps(2)
+    for row in range(1, band):
+        older(row)
+    own_taps(1)
+    hide_rows(0, own)
     wait_rows(1)
-    for j in halo:
-        hide(1, j)
-    acc[...] += taps(1)
+    hide_rows(1, halo)
+    halo_taps(1)
+    own_taps(0)
     wait_rows(0)
-    for j in halo:
-        hide(0, j)
-    acc[...] += taps(0)
+    hide_rows(0, halo)
+    halo_taps(0)
 
     for j in range(band + 2):
-        value = ext[2, band - 1 + j].astype(f32) + acc[pl.ds(j * columns, columns), :] + b3[...]
+        value = ext[2, band - 1 + j].astype(f32) + acc[pl.ds(j * columns, columns), :]
         place = r * band + j - 1
         value = jnp.where((place >= 0) & (place < n_rows * band), value, 0.0)
         for i, part in enumerate(side_by_side(value)):
@@ -297,7 +328,7 @@
                     )
         for i in range(band):
             for lane in range(0, channels, 128):
-                out[2 * i + p, :, pl.ds(lane, 128)] = spread[2 * i + p, lane // 128].astype(bf16)
+                out[0, 2 * i + p, :, pl.ds(lane, 128)] = spread[2 * i + p, lane // 128].astype(bf16)
 
     for k in range(1, n_rows):
         stat1(k).wait_send()
@@ -330,16 +361,22 @@
     n_tm, n_rows = lax.axis_size("tm"), lax.axis_size("rows")
     _, band, columns, channels = frames.shape
     vmem = pl.BlockSpec(memory_space=pltpu.VMEM)
-    anywhere = pl.BlockSpec(memory_space=pl.ANY)
+    hbm = pl.BlockSpec(memory_space=pltpu.HBM)
     dma = pltpu.SemaphoreType.DMA
     return pl.pallas_call(
         functools.partial(kernel, n_tm, n_rows),
-        out_shape=jax.ShapeDtypeStruct((1, 2 * band, 2 * columns, channels), bf16),
+        out_shape=pltpu.VMEM((1, 2 * band, 2 * columns, channels), bf16),
         in_specs=[
-            pl.BlockSpec(memory_space=pltpu.SMEM), vmem, vmem, vmem, anywhere, vmem, anywhere, vmem
-        ],
-        out_specs=pl.BlockSpec((None, 2 * band, 2 * columns, channels), lambda: (0, 0, 0, 0)),
+            hbm
+        ] * 8,
+        out_specs=vmem,
         scratch_shapes=[
+            pltpu.SMEM((n_tm,), jnp.int32),
+            pltpu.VMEM(frames.shape, bf16),
+            pltpu.VMEM((1, channels), f32),
+            pltpu.VMEM((1, channels), f32),
+            pltpu.VMEM((1, channels), f32),
+            pltpu.VMEM((1, channels), f32),
             pltpu.VMEM((3, 3, 3 * channels, channels), bf16),
             pltpu.VMEM((3, 3, channels, channels), bf16),
             pltpu.VMEM((2, 2, 2, 2 * channels, channels), bf16),
@@ -354,14 +391,16 @@
             pltpu.VMEM((n_rows - 1, 8, channels), f32),
             pltpu.VMEM((8, channels), f32),
             pltpu.VMEM((n_tm - 1, 8, channels), f32),
-            dma((2,)),
+            dma((8,)),
             dma((band,)), dma((band,)),
             dma((2, band)), dma((2, band)),
             dma((3, band, 2)), dma((3, band, 2)),
             dma((n_rows - 1,)), dma((n_rows - 1,)),
             dma((n_tm - 1,)), dma((n_tm - 1,)),
         ],
-        compiler_params=pltpu.CompilerParams(collective_id=0, has_side_effects=True),
+        compiler_params=pltpu.CompilerParams(
+            collective_id=0, has_side_effects=True, vmem_limit_bytes=60000000
+        ),
         name="decoder_section",
     )(
         frame_counts, frames, norm_gain[None], norm_bias[None],

time: 25.7 us -> 21.9 us (0.85)
  the two profiles are of different devices: /device:TPU:1 before, /device:TPU:29 now
where the time goes in v2:
time: 21.9 us; the launch traced here: 21.8 us
  Pallas kernels  21 us (96%)
  local copies, waits for them, and re-layouts  0.8 us (4%)
    pallas_call x1, Pallas kernels, body(): pl.pallas_call(functools.partial(kernel, n_tm, n_rows), out_shape=pltpu.V...  21 us
    unnamed x1, local copies, waits for them, and re-layouts  0.8 us

profile of v2, /device:TPU:29, one launch (start us, length us, event | category | flops | bytes accessed | tf_op | source)
XLA Modules:
  0.0 21.8 jit_solution(17837706354879981766)
XLA Ops:
  0.0 21.0 %decoder_section.1 = bf16[1,4,256,256]{3,2,1,0:T(8,128)(2,1)S(1)} custom-call(s32[4]{0:T(128)} %counts_hbm.1, bf16[2,2,128,256]{3,2,1,0:T(8,128)(2,1)} %frames_hbm.1, f32[1,256]{1,0:T(1,128)} %bitcast.6, f32[1,256]{1,0:T(1,128)} %bitcast.7, bf16[3,3,768,256]{3,2,1,0:T(8,128)(2,1)} %bitcast.5, f32[1,256]{1,0:T(1,128)} %bitcast.8, ...), custom_call_target="tpu_custom_call" | custom-call | tf_op jit(solution)/shard_map/decoder_section/pallas_call | solution.py:366
  21.0 0.8 %copy.10 = bf16[1,4,256,256]{3,2,1,0:T(8,128)(2,1)} copy(bf16[1,4,256,256]{3,2,1,0:T(8,128)(2,1)S(1)} %decoder_section.1) | data formatting | bytes 1048576

commit v3 on v2

--- a/solution.py
+++ b/solution.py
@@ -9,6 +9,7 @@
 
 GROUPS = 32
 norm_eps = 1e-06
+HALVES = 2
 MESH = pl.DeviceIdType.MESH
 f32 = jnp.float32
 bf16 = jnp.bfloat16
@@ -48,6 +49,9 @@
     w_sem, sx, rx, sg, rg, sr, rr, s1, r1, s2, r2,
 ):
     band, columns, channels = frames_hbm.shape[1:]
+    halves = HALVES if columns % (16 * HALVES) == 0 else 1
+    span = columns // halves
+    chunks = range(band * halves)
     d = lax.axis_index("tm")
     r = lax.axis_index("rows")
 
@@ -90,32 +94,36 @@
         xsel[row] = jnp.where(own_first, frames[1, row], frames[0, row])
     pl.semaphore_wait(barrier, n_rows - 1 + n_tm - 1)
 
-    def x_copy(row):
+    def piece(ref, row, chunk):
+        return ref.at[row + chunk // halves, pl.ds(chunk % halves * span, span)]
+
+    def x_copy(chunk):
         return pltpu.make_async_remote_copy(
-            src_ref=xsel.at[row], dst_ref=xgot.at[row], send_sem=sx.at[row], recv_sem=rx.at[row],
+            src_ref=piece(xsel, 0, chunk), dst_ref=piece(xgot, 0, chunk),
+            send_sem=sx.at[chunk], recv_sem=rx.at[chunk],
             device_id={"tm": lax.rem(d + 1, n_tm)}, device_id_type=MESH,
         )
 
-    def g_copy(frame, row):
+    def g_copy(frame, chunk):
         return pltpu.make_async_remote_copy(
-            src_ref=ext.at[frame, band + row], dst_ref=ext.at[frame - 1, band + row],
-            send_sem=sg.at[frame - 1, row], recv_sem=rg.at[frame - 1, row],
+            src_ref=piece(ext.at[frame], band, chunk), dst_ref=piece(ext.at[frame - 1], band, chunk),
+            send_sem=sg.at[frame - 1, chunk], recv_sem=rg.at[frame - 1, chunk],
             device_id={"tm": lax.rem(d + 1, n_tm)}, device_id_type=MESH,
         )
 
-    def r_copy(frame, row, down):
+    def r_copy(frame, chunk, down):
         target = lax.rem(r + (1 if down else n_rows - 1), n_rows)
         return pltpu.make_async_remote_copy(
-            src_ref=ext.at[frame, band + row],
-            dst_ref=ext.at[frame, (0 if down else 2 * band) + row],
-            send_sem=sr.at[frame, row, down], recv_sem=rr.at[frame, row, down],
+            src_ref=piece(ext.at[frame], band, chunk),
+            dst_ref=piece(ext.at[frame], 0 if down else 2 * band, chunk),
+            send_sem=sr.at[frame, chunk, down], recv_sem=rr.at[frame, chunk, down],
             device_id={"rows": target}, device_id_type=MESH,
         )
 
     has_next, has_last = d < n_tm - 1, d > 0
     has_above, has_below = r > 0, r < n_rows - 1
-    edge_up = range(2)
-    edge_down = range(band - 2, band)
+    edge_up = range(2 * halves)
+    edge_down = range((band - 2) * halves, band * halves)
 
     def stat1(k):
         return pltpu.make_async_remote_copy(
@@ -131,8 +139,8 @@
 
     @pl.when(has_next)
     def _():
-        for row in range(band):
-            x_copy(row).start()
+        for chunk in chunks:
+            x_copy(chunk).start()
 
     total = jnp.zeros((8, channels), f32)
     square = jnp.zeros((8, channels), f32)
@@ -145,7 +153,7 @@
     total = jnp.sum(total, axis=0, keepdims=True)
     square = jnp.sum(square, axis=0, keepdims=True)
     mine[...] = jnp.concatenate(
-        [jnp.broadcast_to(total, (4, channels)), jnp.broadcast_to(square, (4, channels))], axis=0
+        [total, square], axis=0
     )
     for k in range(1, n_rows):
         stat1(k).start()
@@ -166,36 +174,37 @@
                         summed.astype(bf16)
                     )
 
-    def send_rows(frame, row):
+    def send_rows(frame, chunk):
         @pl.when(has_above)
         def _():
-            if row in edge_up:
-                r_copy(frame, row, 0).start()
+            if chunk in edge_up:
+                r_copy(frame, chunk, 0).start()
 
         @pl.when(has_below)
         def _():
-            if row in edge_down:
-                r_copy(frame, row, 1).start()
-
-    for row in range(band):
+            if chunk in edge_down:
+                r_copy(frame, chunk, 1).start()
+
+    for chunk in chunks:
+        row, cells = chunk // halves, pl.ds(chunk % halves * span, span)
+
         @pl.when(has_last)
         def _():
-            x_copy(row).wait_recv()
-            ext[2, band + row] = jnp.where(own_first, frames[0, row], xgot[row])
+            x_copy(chunk).wait_recv()
+            ext[2, band + row, cells] = jnp.where(own_first, frames[0, row, cells], xgot[row, cells])
 
         @pl.when(d == 0)
         def _():
-            ext[2, band + row] = frames[0, row]
-            ext[1, band + row] = frames[0, row]
-            ext[0, band + row] = frames[0, row]
+            for frame in range(3):
+                ext[frame, band + row, cells] = frames[0, row, cells]
 
         @pl.when(has_next)
         def _():
-            g_copy(2, row).start()
-
-        send_rows(2, row)
-
-        if row == 0:
+            g_copy(2, chunk).start()
+
+        send_rows(2, chunk)
+
+        if chunk == halves - 1:
             for k in range(1, n_rows):
                 stat1(k).wait_recv()
             plane_sum = mine[...]
@@ -205,16 +214,16 @@
             for k in range(1, n_tm):
                 stat2(k).start()
 
-    for row in range(band):
+    for chunk in chunks:
         @pl.when(has_last)
         def _():
-            g_copy(2, row).wait_recv()
+            g_copy(2, chunk).wait_recv()
 
         @pl.when(has_next)
         def _():
-            g_copy(1, row).start()
-
-        send_rows(1, row)
+            g_copy(1, chunk).start()
+
+        send_rows(1, chunk)
 
     for k in range(1, n_tm):
         stat2(k).wait_recv()
@@ -223,7 +232,7 @@
         whole = whole + tm_stats[k - 1]
     width = channels // GROUPS
     whole = group_total(whole, width) / float(n_tm * n_rows * band * columns * width)
-    mean, mean_square = whole[0:1], whole[4:5]
+    mean, mean_square = whole[0:1], whole[1:2]
     inverse = lax.rsqrt(mean_square - mean * mean + norm_eps)
     for load in small:
         load.wait()
@@ -246,13 +255,13 @@
     def wait_rows(frame):
         @pl.when(has_below)
         def _():
-            for row in edge_up:
-                r_copy(frame, row, 0).wait_recv()
+            for chunk in edge_up:
+                r_copy(frame, chunk, 0).wait_recv()
 
         @pl.when(has_above)
         def _():
-            for row in edge_down:
-                r_copy(frame, row, 1).wait_recv()
+            for chunk in edge_down:
+                r_copy(frame, chunk, 1).wait_recv()
 
     def tap(frame, k, first, rows):
         return jnp.dot(
@@ -278,24 +287,23 @@
         for j in rows:
             hide(frame, j)
 
-    def older(row):
+    def older(chunk):
         @pl.when(has_last)
         def _():
-            g_copy(1, row).wait_recv()
-
-        send_rows(0, row)
+            g_copy(1, chunk).wait_recv()
+
+        send_rows(0, chunk)
 
     acc[...] = jnp.zeros(acc.shape, f32) + b3[...]
     hide_rows(2, own)
     load3.wait()
     own_taps(2)
-    hide_rows(1, own)
-    older(0)
+    for chunk in chunks:
+        older(chunk)
     wait_rows(2)
     hide_rows(2, halo)
     halo_taps(2)
-    for row in range(1, band):
-        older(row)
+    hide_rows(1, own)
     own_taps(1)
     hide_rows(0, own)
     wait_rows(1)
@@ -337,22 +345,22 @@
 
     @pl.when(has_next)
     def _():
-        for row in range(band):
-            x_copy(row).wait_send()
-            g_copy(2, row).wait_send()
-            g_copy(1, row).wait_send()
+        for chunk in chunks:
+            x_copy(chunk).wait_send()
+            g_copy(2, chunk).wait_send()
+            g_copy(1, chunk).wait_send()
 
     @pl.when(has_above)
     def _():
         for frame in range(3):
-            for row in edge_up:
-                r_copy(frame, row, 0).wait_send()
+            for chunk in edge_up:
+                r_copy(frame, chunk, 0).wait_send()
 
     @pl.when(has_below)
     def _():
         for frame in range(3):
-            for row in edge_down:
-                r_copy(frame, row, 1).wait_send()
+            for chunk in edge_down:
+                r_copy(frame, chunk, 1).wait_send()
 
 
 def body(
@@ -387,14 +395,14 @@
             pltpu.VMEM(((band + 2) * columns, channels), f32),
             pltpu.VMEM(((band + 2) * columns, 3 * channels), bf16),
             pltpu.VMEM((2 * band, channels // 128, 2 * columns, 128), f32),
-            pltpu.VMEM((8, channels), f32),
-            pltpu.VMEM((n_rows - 1, 8, channels), f32),
-            pltpu.VMEM((8, channels), f32),
-            pltpu.VMEM((n_tm - 1, 8, channels), f32),
+            pltpu.VMEM((2, channels), f32),
+            pltpu.VMEM((n_rows - 1, 2, channels), f32),
+            pltpu.VMEM((2, channels), f32),
+            pltpu.VMEM((n_tm - 1, 2, channels), f32),
             dma((8,)),
-            dma((band,)), dma((band,)),
-            dma((2, band)), dma((2, band)),
-            dma((3, band, 2)), dma((3, band, 2)),
+            dma((HALVES * band,)), dma((HALVES * band,)),
+            dma((2, HALVES * band)), dma((2, HALVES * band)),
+            dma((3, HALVES * band, 2)), dma((3, HALVES * band, 2)),
             dma((n_rows - 1,)), dma((n_rows - 1,)),
             dma((n_tm - 1,)), dma((n_tm - 1,)),
         ],

time: 21.9 us -> 21.1 us (0.963)
  the two profiles are of different devices: /device:TPU:29 before, /device:TPU:1 now
where the time goes in v3:
time: 21.1 us; the launch traced here: 21 us
  Pallas kernels  20.2 us (96%)
  local copies, waits for them, and re-layouts  0.8 us (4%)
    pallas_call x1, Pallas kernels, body(): pl.pallas_call(functools.partial(kernel, n_tm, n_rows), out_shape=pltpu.V...  20.2 us
    unnamed x1, local copies, waits for them, and re-layouts  0.8 us

profile of v3, /device:TPU:1, one launch (start us, length us, event | category | flops | bytes accessed | tf_op | source)
XLA Modules:
  0.0 21.0 jit_solution(7257770661502434857)
XLA Ops:
  0.0 20.2 %decoder_section.1 = bf16[1,4,256,256]{3,2,1,0:T(8,128)(2,1)S(1)} custom-call(s32[4]{0:T(128)} %counts_hbm.1, bf16[2,2,128,256]{3,2,1,0:T(8,128)(2,1)} %frames_hbm.1, f32[1,256]{1,0:T(1,128)} %bitcast.6, f32[1,256]{1,0:T(1,128)} %bitcast.7, bf16[3,3,768,256]{3,2,1,0:T(8,128)(2,1)} %bitcast.5, f32[1,256]{1,0:T(1,128)} %bitcast.8, ...), custom_call_target="tpu_custom_call" | custom-call | tf_op jit(solution)/shard_map/decoder_section/pallas_call | solution.py:374
  20.2 0.8 %copy.10 = bf16[1,4,256,256]{3,2,1,0:T(8,128)(2,1)} copy(bf16[1,4,256,256]{3,2,1,0:T(8,128)(2,1)S(1)} %decoder_section.1) | data formatting | bytes 1048576
